TPU v7x, 32 devices: a whole 2x2x4 slice. The times are simulated.
32 devices in a mesh: blk: 16 (over z, y, x), grp: 2 (over core).
Axes of the slice: x: 2, y: 2, z: 4, core: 2. Of those that a mesh axis runs over, the one named last changes fastest.
Arguments:
- schur_blocks: bfloat16 [64, 1024, 1024], P(('blk', 'grp')), may hold values from -1 to 5, as said below
- residual: float32 [64, 1024, 128], P(('blk', 'grp')), may hold values from -200 to 200
- direction: float32 [64, 1024, 128], P(('blk', 'grp')), may hold values from -200 to 200
- corner_map: int32 [64, 24], P(('blk', 'grp')), may hold values from 0 to 511
- panel_order: int32 [8], replicated, may hold values from 0 to 7, each once
- coarse_factor: float32 [8, 8, 1024, 1024], P(None, None, 'blk'), may hold values from -0.0625 to 0.0625
- block_inverses: float32 [8, 1024, 1024], P(None, 'blk'), may hold values from -0.1875 to 0.1875
Outputs:
- residual_next: float32 [64, 1024, 128], P(('blk', 'grp'))
- direction_next: float32 [64, 1024, 128], P(('blk', 'grp'))
Inputs may be any that keep to these rules, and one draw needn't show every extreme that they name: `schur_blocks`: each subdomain's block is symmetric positive definite. `panel_order`: each coarse block appears once.
All inputs are finite; a program needn't handle non-finite values.
Results may differ from a plain program's by a relative error of at most 0.0048.
Values sent between devices are 32-bit elements; how exact they have to be, the bound alone decides.
No kernel may reach another device: no remote copies, remote signals or barrier semaphores. Data moves between devices by JAX's collectives and lax.ppermute only.
A program may use at most 64 MiB of HBM per device.

v0:
```python
import jax
import jax.numpy as jnp
from jax import lax
from jax.sharding import PartitionSpec as P

PANELS = 8
precise = lax.Precision.HIGHEST


def squares(residual):
    return lax.psum(jnp.sum(residual * residual, axis=(0, 1)), ("blk", "grp"))


def solve(coarse, panel_order, coarse_factor, block_inverses):
    pending = jnp.zeros_like(coarse)
    solved = jnp.zeros_like(coarse)
    for position in range(PANELS):
        current = panel_order[position]
        target = lax.dynamic_index_in_dim(coarse - pending, current, 0, keepdims=False)
        inverse = lax.dynamic_index_in_dim(block_inverses, current, 0, keepdims=False)
        block_value = jnp.dot(
            inverse,
            lax.all_gather(target, "blk", axis=0, tiled=True),
            precision=precise,
            preferred_element_type=jnp.float32,
        )
        solved = lax.dynamic_update_index_in_dim(solved, block_value, current, 0)
        if position + 1 < PANELS:
            coupling = lax.dynamic_index_in_dim(coarse_factor, current, 1, keepdims=False)
            pending = pending + jnp.einsum(
                "aic,cv->aiv",
                coupling,
                lax.all_gather(block_value, "blk", axis=0, tiled=True),
                precision=precise,
            )
    return solved


def local(
    schur_blocks, residual, direction, corner_map, panel_order, coarse_factor, block_inverses
):
    panels = block_inverses.shape[0]
    rows_b = block_inverses.shape[1]
    sub_count = schur_blocks.shape[0]
    corners = corner_map.shape[1]
    columns_iota = lax.broadcasted_iota(jnp.int32, (sub_count, corners, panels * rows_b), 2)
    placing = (corner_map[:, :, None] == columns_iota).astype(jnp.float32)
    norm_now = squares(residual)
    applied = jnp.einsum(
        "sij,sjv->siv",
        schur_blocks,
        direction.astype(jnp.bfloat16),
        preferred_element_type=jnp.float32,
    )
    curvature = lax.psum(jnp.sum(direction * applied, axis=(0, 1)), ("blk", "grp"))
    step_size = norm_now / curvature
    residual = residual - step_size * applied
    norm_next = squares(residual)
    corner_part = jnp.einsum("scm,scv->mv", placing, residual[:, :corners, :], precision=precise)
    corner_part = corner_part.reshape(panels, rows_b, -1)
    coarse_part = lax.psum(corner_part, "grp")
    solved = solve(coarse_part, panel_order, coarse_factor, block_inverses)
    flat_solved = solved.reshape(panels * rows_b, -1)
    correction = jnp.einsum("scm,mv->scv", placing, flat_solved, precision=precise)
    corrected = jnp.concatenate(
        [residual[:, :corners, :] + correction, residual[:, corners:, :]], axis=1
    )
    direction = corrected + norm_next / norm_now * direction
    return (residual, direction)


def solution(mesh):
    in_specs = (
        P(("blk", "grp"), None, None),
        P(("blk", "grp"), None, None),
        P(("blk", "grp"), None, None),
        P(("blk", "grp"), None),
        P(),
        P(None, None, "blk", None),
        P(None, "blk", None),
    )
    out_specs = (P(("blk", "grp"), None, None), P(("blk", "grp"), None, None))
    return jax.shard_map(local, mesh=mesh, in_specs=in_specs, out_specs=out_specs, check_vma=False)
```

profile of v0, /device:TPU:0, one launch (start us, length us, event | category | flops | bytes accessed | tf_op | source)
XLA Modules:
  0.0 743.4 jit_solution(7819238958384494164)
XLA Ops:
  7.2 0.0 copy-start
  7.2 0.0 all-reduce.3.cloned.1.call-start
  7.2 1.6 multiply_reduce_fusion.2
  8.9 5.0 multiply_reduce_fusion.1
  13.9 41.9 %all-reduce = (f32[128]{0:T(128)S(1)}, f32[128]{0:T(128)S(1)}) all-reduce(f32[128]{0:T(128)S(1)} %multiply_reduce_fusion.2, f32[128]{0:T(128)S(1)} %get-tuple-element.14), channel_id=1, replica_groups=mesh['blk'=16,'grp'=2] {'blk','grp'}, use_global_device_ids=true, to_apply=%region_1.0 | all-reduce | flops 256 | bytes 2048 | tf_op jit(solution)/shard_map/psum | solution.py:11
  55.8 1.8 multiply_reduce_fusion
  57.7 0.0 copy-done.7
  57.7 1.2 fusion.77
  58.8 0.0 all-reduce.3.cloned.1.call-update
  58.9 0.7 fusion.96
  69.5 1.0 slice.42
  70.6 40.0 %psum.31 = f32[128]{0:T(128)S(1)} all-reduce(f32[128]{0:T(128)S(1)} %get-tuple-element.4), channel_id=1, replica_groups=mesh['blk'=16,'grp'=2] {'blk','grp'}, use_global_device_ids=true, to_apply=%region_6.0 | all-reduce | flops 128 | bytes 1024 | tf_op jit(solution)/shard_map/psum | solution.py:11
  115.6 0.0 all-reduce.3.cloned.1.call-done
  115.7 0.8 constant_dynamic-slice_fusion
  116.4 43.7 %all-gather = f32[1,1024,128]{2,1,0:T(8,128)S(1)} all-gather(f32[1,64,128]{2,1,0:T(8,128)S(1)} %constant_dynamic-slice_fusion), channel_id=2, replica_groups=mesh['blk'=16,'grp'=2] {'blk'}, dimensions={1}, use_global_device_ids=true | all-gather | bytes 557056 | tf_op jit(solution)/shard_map/all_gather | solution.py:23
  160.2 0.0 copy-start.1
  160.2 0.5 bitcast_dynamic-update-slice_fusion.6
  160.7 38.5 %all_gather.46 = f32[1024,128]{1,0:T(8,128)S(1)} all-gather(f32[64,128]{1,0:T(8,128)S(1)} %get-tuple-element.17), channel_id=1, replica_groups=mesh['blk'=16,'grp'=2] {'blk'}, dimensions={0}, use_global_device_ids=true | all-gather | bytes 557056 | tf_op jit(solution)/shard_map/all_gather | solution.py:33
  199.2 3.4 fusion.12
  202.6 0.0 copy-done.5
  202.6 40.7 %all-gather.1 = f32[1,1024,128]{2,1,0:T(8,128)S(1)} all-gather(f32[1,64,128]{2,1,0:T(8,128)S(1)} %dynamic-slice_subtract_fusion.6), channel_id=3, replica_groups=mesh['blk'=16,'grp'=2] {'blk'}, dimensions={1}, use_global_device_ids=true | all-gather | bytes 557056 | tf_op jit(solution)/shard_map/all_gather | solution.py:23
  243.3 0.5 bitcast_dynamic-update-slice_fusion.5
  243.8 38.6 %all_gather.48 = f32[1024,128]{1,0:T(8,128)S(1)} all-gather(f32[64,128]{1,0:T(8,128)S(1)} %get-tuple-element.19), channel_id=1, replica_groups=mesh['blk'=16,'grp'=2] {'blk'}, dimensions={0}, use_global_device_ids=true | all-gather | bytes 557056 | tf_op jit(solution)/shard_map/all_gather | solution.py:33
  282.4 3.4 fusion.21
  285.8 40.3 %all-gather.2 = f32[1,1024,128]{2,1,0:T(8,128)S(1)} all-gather(f32[1,64,128]{2,1,0:T(8,128)S(1)} %dynamic-slice_subtract_fusion.5), channel_id=4, replica_groups=mesh['blk'=16,'grp'=2] {'blk'}, dimensions={1}, use_global_device_ids=true | all-gather | bytes 557056 | tf_op jit(solution)/shard_map/all_gather | solution.py:23
  326.1 0.5 bitcast_dynamic-update-slice_fusion.4
  326.6 38.6 %all_gather.50 = f32[1024,128]{1,0:T(8,128)S(1)} all-gather(f32[64,128]{1,0:T(8,128)S(1)} %get-tuple-element.21), channel_id=1, replica_groups=mesh['blk'=16,'grp'=2] {'blk'}, dimensions={0}, use_global_device_ids=true | all-gather | bytes 557056 | tf_op jit(solution)/shard_map/all_gather | solution.py:33
  365.2 3.4 fusion.24
  368.6 41.1 %all-gather.3 = f32[1,1024,128]{2,1,0:T(8,128)S(1)} all-gather(f32[1,64,128]{2,1,0:T(8,128)S(1)} %dynamic-slice_subtract_fusion.4), channel_id=5, replica_groups=mesh['blk'=16,'grp'=2] {'blk'}, dimensions={1}, use_global_device_ids=true | all-gather | bytes 557056 | tf_op jit(solution)/shard_map/all_gather | solution.py:23
  409.8 0.5 bitcast_dynamic-update-slice_fusion.3
  410.2 38.3 %all_gather.52 = f32[1024,128]{1,0:T(8,128)S(1)} all-gather(f32[64,128]{1,0:T(8,128)S(1)} %get-tuple-element.23), channel_id=1, replica_groups=mesh['blk'=16,'grp'=2] {'blk'}, dimensions={0}, use_global_device_ids=true | all-gather | bytes 557056 | tf_op jit(solution)/shard_map/all_gather | solution.py:33
  448.5 1.8 fusion.27
  450.3 40.8 %all-gather.4 = f32[1,1024,128]{2,1,0:T(8,128)S(1)} all-gather(f32[1,64,128]{2,1,0:T(8,128)S(1)} %dynamic-slice_subtract_fusion.3), channel_id=6, replica_groups=mesh['blk'=16,'grp'=2] {'blk'}, dimensions={1}, use_global_device_ids=true | all-gather | bytes 557056 | tf_op jit(solution)/shard_map/all_gather | solution.py:23
  491.1 0.5 bitcast_dynamic-update-slice_fusion.2
  491.6 38.6 %all_gather.54 = f32[1024,128]{1,0:T(8,128)S(1)} all-gather(f32[64,128]{1,0:T(8,128)S(1)} %get-tuple-element.25), channel_id=1, replica_groups=mesh['blk'=16,'grp'=2] {'blk'}, dimensions={0}, use_global_device_ids=true | all-gather | bytes 557056 | tf_op jit(solution)/shard_map/all_gather | solution.py:33
  530.2 1.8 fusion.30
  532.0 40.5 %all-gather.5 = f32[1,1024,128]{2,1,0:T(8,128)S(1)} all-gather(f32[1,64,128]{2,1,0:T(8,128)S(1)} %dynamic-slice_subtract_fusion.2), channel_id=7, replica_groups=mesh['blk'=16,'grp'=2] {'blk'}, dimensions={1}, use_global_device_ids=true | all-gather | bytes 557056 | tf_op jit(solution)/shard_map/all_gather | solution.py:23
  572.5 0.4 bitcast_dynamic-update-slice_fusion.1
  573.0 38.5 %all_gather.56 = f32[1024,128]{1,0:T(8,128)S(1)} all-gather(f32[64,128]{1,0:T(8,128)S(1)} %get-tuple-element.27), channel_id=1, replica_groups=mesh['blk'=16,'grp'=2] {'blk'}, dimensions={0}, use_global_device_ids=true | all-gather | bytes 557056 | tf_op jit(solution)/shard_map/all_gather | solution.py:33
  611.4 1.8 fusion.33
  613.3 40.4 %all-gather.6 = f32[1,1024,128]{2,1,0:T(8,128)S(1)} all-gather(f32[1,64,128]{2,1,0:T(8,128)S(1)} %dynamic-slice_subtract_fusion.1), channel_id=8, replica_groups=mesh['blk'=16,'grp'=2] {'blk'}, dimensions={1}, use_global_device_ids=true | all-gather | bytes 557056 | tf_op jit(solution)/shard_map/all_gather | solution.py:23
  653.6 0.5 bitcast_dynamic-update-slice_fusion
  654.1 38.3 %all_gather.58 = f32[1024,128]{1,0:T(8,128)S(1)} all-gather(f32[64,128]{1,0:T(8,128)S(1)} %get-tuple-element.29), channel_id=1, replica_groups=mesh['blk'=16,'grp'=2] {'blk'}, dimensions={0}, use_global_device_ids=true | all-gather | bytes 557056 | tf_op jit(solution)/shard_map/all_gather | solution.py:33
  692.4 1.8 fusion
  694.2 40.5 %all-gather.7 = f32[1,1024,128]{2,1,0:T(8,128)S(1)} all-gather(f32[1,64,128]{2,1,0:T(8,128)S(1)} %dynamic-slice_subtract_fusion), channel_id=9, replica_groups=mesh['blk'=16,'grp'=2] {'blk'}, dimensions={1}, use_global_device_ids=true | all-gather | bytes 557056 | tf_op jit(solution)/shard_map/all_gather | solution.py:23
  734.7 0.5 fusion.36
  735.2 0.2 convolution_add_fusion
  735.4 1.1 maximum_add_fusion
  (22 shorter events, 0.1 us)
Async XLA Ops:
  7.2 153.0 %copy-start = (f32[8,64,1024]{2,1,0:T(8,128)S(1)}, f32[8,64,1024]{2,1,0:T(8,128)}, u32[]{:S(2)}) copy-start(f32[8,64,1024]{2,1,0:T(8,128)} %param.13) | copy-start | bytes 6291460
  7.2 108.5 %all-reduce.3.cloned.1.call-start = ((), (), s32[]{:S(2)}) async-start(), calls=%async_computation | async-start | bytes 524288 | tf_op jit(solution)/shard_map/psum | solution.py:61
  13.9 43.8 %copy-start.7 = (s32[2,24]{1,0:T(2,128)S(1)}, s32[2,24]{1,0:T(2,128)}, u32[]{:S(2)}) copy-start(s32[2,24]{1,0:T(2,128)} %param.10) | copy-start | bytes 580
  13.9 45.0 %copy-start.6 = (s32[8]{0:T(128)S(1)}, s32[8]{0:T(128)}, u32[]{:S(2)}) copy-start(s32[8]{0:T(128)} %param.11) | copy-start | bytes 100
  57.6 677.5 %copy-start.2 = (f32[2,1024,128]{2,1,0:T(8,128)}, f32[2,1024,128]{2,1,0:T(8,128)S(1)}, u32[]{:S(2)}) copy-start(f32[2,1024,128]{2,1,0:T(8,128)S(1)} %get-tuple-element.5) | copy-start | bytes 3145732
  160.2 42.4 %copy-start.5 = (f32[8,64,128]{2,1,0:T(8,128)S(1)}, f32[8,64,128]{2,1,0:T(8,128)}, u32[]{:S(2)}) copy-start(f32[8,64,128]{2,1,0:T(8,128)} %all-reduce.3.cloned.1.call-done) | copy-start | bytes 786436
  160.2 288.3 %copy-start.1 = (f32[8,8,64,1024]{3,2,1,0:T(8,128)S(1)}, f32[8,8,64,1024]{3,2,1,0:T(8,128)}, u32[]{:S(2)}) copy-start(f32[8,8,64,1024]{3,2,1,0:T(8,128)} %param.12) | copy-start | bytes 50331652
  692.4 43.1 %copy-start.3 = (f32[2,1024,128]{2,1,0:T(8,128)S(1)}, f32[2,1024,128]{2,1,0:T(8,128)}, u32[]{:S(2)}) copy-start(f32[2,1024,128]{2,1,0:T(8,128)} %param.9) | copy-start | bytes 3145732
  692.4 43.1 %copy-start.4 = (f32[2,1000,128]{2,1,0:T(8,128)S(1)}, f32[2,1000,128]{2,1,0:T(8,128)}, u32[]{:S(2)}) copy-start(f32[2,1000,128]{2,1,0:T(8,128)} %slice.42) | copy-start | bytes 3072004
Sparse Core Ops, SparseCore 0:
  59.0 18.0 all-reduce.2
where the time goes:
time: 744 us; the launch traced here: 743 us
  blocking collectives  679 us (91%)
  between operations  29.3 us (4%)
  matrix products  27.4 us (4%)
    all_gather x8, blocking collectives, solve(): lax.all_gather(target, 'blk', axis=0, tiled=True)  328 us
    all_gather x7, blocking collectives, solve(): lax.all_gather(block_value, 'blk', axis=0, tiled=True)  269 us
    psum x2, blocking collectives, squares(): return lax.psum(jnp.sum(residual * residual, axis=(0, 1)), ('blk', 'grp'))  82 us
    dot_general x7, matrix products, solve(): jnp.einsum('aic,cv->aiv', coupling, lax.all_gather(block_value, 'blk', ax...  17.4 us
  transfers between devices with their start and end apart: 1, of which 0 were waited for; matrix products, arithmetic and copies ran while one was open for 0% of the time, Pallas kernels for 0%

commit v1 on v0

--- a/solution.py
+++ b/solution.py
@@ -8,7 +8,7 @@
 
 
 def squares(residual):
-    return lax.psum(jnp.sum(residual * residual, axis=(0, 1)), ("blk", "grp"))
+    return lax.psum(lax.psum(jnp.sum(residual * residual, axis=(0, 1)), "grp"), "blk")
 
 
 def solve(coarse, panel_order, coarse_factor, block_inverses):

time: 744 us -> 783 us (1.052)
  blocking collectives: 679 us -> 718 us
    psum x2 -> x5, blocking collectives: 82 us -> 125 us  [the longest x2 83.3 us: squares(): lax.psum(lax.psum(jnp.sum(residual * residual, axis=(0, 1)), 'grp'), 'blk')]
    all_gather x8, blocking collectives: 328 us -> 308 us  [solve(): lax.all_gather(target, 'blk', axis=0, tiled=True)]
    all_gather x7, blocking collectives: 269 us -> 285 us  [solve(): lax.all_gather(block_value, 'blk', axis=0, tiled=True)]
where the time goes in v1:
time: 783 us; the launch traced here: 782 us
  blocking collectives  718 us (92%)
  between operations  29.2 us (4%)
  matrix products  27.4 us (3%)
    all_gather x8, blocking collectives, solve(): lax.all_gather(target, 'blk', axis=0, tiled=True)  308 us
    all_gather x7, blocking collectives, solve(): lax.all_gather(block_value, 'blk', axis=0, tiled=True)  285 us
    psum x2, blocking collectives, squares(): lax.psum(lax.psum(jnp.sum(residual * residual, axis=(0, 1)), 'grp'), 'blk')  83.3 us
    psum x1, blocking collectives, local(): lax.psum(jnp.sum(direction * applied, axis=(0, 1)), ('blk', 'grp'))  36.8 us
    dot_general x7, matrix products, solve(): jnp.einsum('aic,cv->aiv', coupling, lax.all_gather(block_value, 'blk', ax...  17.4 us
  transfers between devices with their start and end apart: 1, of which 0 were waited for; matrix products, arithmetic and copies ran while one was open for 0% of the time, Pallas kernels for 0%

profile of v1, /device:TPU:0, one launch (start us, length us, event | category | flops | bytes accessed | tf_op | source)
XLA Modules:
  0.0 781.9 jit_solution(6791802455828723292)
XLA Ops:
  7.2 0.0 copy-start
  7.2 0.0 all-reduce.2.cloned.1.call-start
  7.2 1.6 multiply_reduce_fusion.2
  8.9 2.6 psum.42
  11.5 43.3 %psum.43 = f32[128]{0:T(128)S(1)} all-reduce(f32[128]{0:T(128)S(1)} %psum.42), channel_id=1, replica_groups=mesh['blk'=16,'grp'=2] {'blk'}, use_global_device_ids=true, to_apply=%region_2.0 | all-reduce | flops 128 | bytes 1024 | tf_op jit(solution)/shard_map/psum | solution.py:11
  54.8 5.0 multiply_reduce_fusion.1
  59.8 36.8 %psum.44 = f32[128]{0:T(128)S(1)} all-reduce(f32[128]{0:T(128)S(1)} %get-tuple-element.12), channel_id=1, replica_groups=mesh['blk'=16,'grp'=2] {'blk','grp'}, use_global_device_ids=true, to_apply=%region_4.0 | all-reduce | flops 128 | bytes 1024 | tf_op jit(solution)/shard_map/psum | solution.py:55
  96.6 1.8 multiply_reduce_fusion
  98.5 1.2 fusion.77
  99.6 0.0 all-reduce.2.cloned.1.call-update
  99.7 0.7 fusion.96
  110.3 1.0 slice.42
  111.4 2.4 psum.46
  113.8 40.0 %psum.47 = f32[128]{0:T(128)S(1)} all-reduce(f32[128]{0:T(128)S(1)} %psum.46), channel_id=1, replica_groups=mesh['blk'=16,'grp'=2] {'blk'}, use_global_device_ids=true, to_apply=%region_8.0 | all-reduce | flops 128 | bytes 1024 | tf_op jit(solution)/shard_map/psum | solution.py:11
  158.8 0.0 all-reduce.2.cloned.1.call-done
  158.8 0.8 constant_dynamic-slice_fusion
  159.6 38.6 %all-gather = f32[1,1024,128]{2,1,0:T(8,128)S(1)} all-gather(f32[1,64,128]{2,1,0:T(8,128)S(1)} %constant_dynamic-slice_fusion), channel_id=2, replica_groups=mesh['blk'=16,'grp'=2] {'blk'}, dimensions={1}, use_global_device_ids=true | all-gather | bytes 557056 | tf_op jit(solution)/shard_map/all_gather | solution.py:23
  198.2 0.5 bitcast_dynamic-update-slice_fusion.6
  198.7 40.8 %all_gather.46 = f32[1024,128]{1,0:T(8,128)S(1)} all-gather(f32[64,128]{1,0:T(8,128)S(1)} %get-tuple-element.15), channel_id=1, replica_groups=mesh['blk'=16,'grp'=2] {'blk'}, dimensions={0}, use_global_device_ids=true | all-gather | bytes 557056 | tf_op jit(solution)/shard_map/all_gather | solution.py:33
  239.5 3.4 fusion.12
  242.9 38.4 %all-gather.1 = f32[1,1024,128]{2,1,0:T(8,128)S(1)} all-gather(f32[1,64,128]{2,1,0:T(8,128)S(1)} %dynamic-slice_subtract_fusion.6), channel_id=3, replica_groups=mesh['blk'=16,'grp'=2] {'blk'}, dimensions={1}, use_global_device_ids=true | all-gather | bytes 557056 | tf_op jit(solution)/shard_map/all_gather | solution.py:23
  281.3 0.5 bitcast_dynamic-update-slice_fusion.5
  281.8 40.5 %all_gather.48 = f32[1024,128]{1,0:T(8,128)S(1)} all-gather(f32[64,128]{1,0:T(8,128)S(1)} %get-tuple-element.17), channel_id=1, replica_groups=mesh['blk'=16,'grp'=2] {'blk'}, dimensions={0}, use_global_device_ids=true | all-gather | bytes 557056 | tf_op jit(solution)/shard_map/all_gather | solution.py:33
  322.3 3.4 fusion.21
  325.7 38.5 %all-gather.2 = f32[1,1024,128]{2,1,0:T(8,128)S(1)} all-gather(f32[1,64,128]{2,1,0:T(8,128)S(1)} %dynamic-slice_subtract_fusion.5), channel_id=4, replica_groups=mesh['blk'=16,'grp'=2] {'blk'}, dimensions={1}, use_global_device_ids=true | all-gather | bytes 557056 | tf_op jit(solution)/shard_map/all_gather | solution.py:23
  364.2 0.5 bitcast_dynamic-update-slice_fusion.4
  364.6 40.7 %all_gather.50 = f32[1024,128]{1,0:T(8,128)S(1)} all-gather(f32[64,128]{1,0:T(8,128)S(1)} %get-tuple-element.19), channel_id=1, replica_groups=mesh['blk'=16,'grp'=2] {'blk'}, dimensions={0}, use_global_device_ids=true | all-gather | bytes 557056 | tf_op jit(solution)/shard_map/all_gather | solution.py:33
  405.3 3.4 fusion.24
  408.7 38.6 %all-gather.3 = f32[1,1024,128]{2,1,0:T(8,128)S(1)} all-gather(f32[1,64,128]{2,1,0:T(8,128)S(1)} %dynamic-slice_subtract_fusion.4), channel_id=5, replica_groups=mesh['blk'=16,'grp'=2] {'blk'}, dimensions={1}, use_global_device_ids=true | all-gather | bytes 557056 | tf_op jit(solution)/shard_map/all_gather | solution.py:23
  447.4 0.5 bitcast_dynamic-update-slice_fusion.3
  447.8 41.1 %all_gather.52 = f32[1024,128]{1,0:T(8,128)S(1)} all-gather(f32[64,128]{1,0:T(8,128)S(1)} %get-tuple-element.21), channel_id=1, replica_groups=mesh['blk'=16,'grp'=2] {'blk'}, dimensions={0}, use_global_device_ids=true | all-gather | bytes 557056 | tf_op jit(solution)/shard_map/all_gather | solution.py:33
  488.9 1.8 fusion.27
  490.8 38.6 %all-gather.4 = f32[1,1024,128]{2,1,0:T(8,128)S(1)} all-gather(f32[1,64,128]{2,1,0:T(8,128)S(1)} %dynamic-slice_subtract_fusion.3), channel_id=6, replica_groups=mesh['blk'=16,'grp'=2] {'blk'}, dimensions={1}, use_global_device_ids=true | all-gather | bytes 557056 | tf_op jit(solution)/shard_map/all_gather | solution.py:23
  529.3 0.5 bitcast_dynamic-update-slice_fusion.2
  529.8 40.8 %all_gather.54 = f32[1024,128]{1,0:T(8,128)S(1)} all-gather(f32[64,128]{1,0:T(8,128)S(1)} %get-tuple-element.23), channel_id=1, replica_groups=mesh['blk'=16,'grp'=2] {'blk'}, dimensions={0}, use_global_device_ids=true | all-gather | bytes 557056 | tf_op jit(solution)/shard_map/all_gather | solution.py:33
  570.6 1.8 fusion.30
  572.4 38.6 %all-gather.5 = f32[1,1024,128]{2,1,0:T(8,128)S(1)} all-gather(f32[1,64,128]{2,1,0:T(8,128)S(1)} %dynamic-slice_subtract_fusion.2), channel_id=7, replica_groups=mesh['blk'=16,'grp'=2] {'blk'}, dimensions={1}, use_global_device_ids=true | all-gather | bytes 557056 | tf_op jit(solution)/shard_map/all_gather | solution.py:23
  611.0 0.5 bitcast_dynamic-update-slice_fusion.1
  611.5 40.7 %all_gather.56 = f32[1024,128]{1,0:T(8,128)S(1)} all-gather(f32[64,128]{1,0:T(8,128)S(1)} %get-tuple-element.25), channel_id=1, replica_groups=mesh['blk'=16,'grp'=2] {'blk'}, dimensions={0}, use_global_device_ids=true | all-gather | bytes 557056 | tf_op jit(solution)/shard_map/all_gather | solution.py:33
  652.2 1.8 fusion.33
  654.0 38.4 %all-gather.6 = f32[1,1024,128]{2,1,0:T(8,128)S(1)} all-gather(f32[1,64,128]{2,1,0:T(8,128)S(1)} %dynamic-slice_subtract_fusion.1), channel_id=8, replica_groups=mesh['blk'=16,'grp'=2] {'blk'}, dimensions={1}, use_global_device_ids=true | all-gather | bytes 557056 | tf_op jit(solution)/shard_map/all_gather | solution.py:23
  692.4 0.5 bitcast_dynamic-update-slice_fusion
  692.9 40.3 %all_gather.58 = f32[1024,128]{1,0:T(8,128)S(1)} all-gather(f32[64,128]{1,0:T(8,128)S(1)} %get-tuple-element.27), channel_id=1, replica_groups=mesh['blk'=16,'grp'=2] {'blk'}, dimensions={0}, use_global_device_ids=true | all-gather | bytes 557056 | tf_op jit(solution)/shard_map/all_gather | solution.py:33
  733.2 1.8 fusion
  735.0 38.3 %all-gather.7 = f32[1,1024,128]{2,1,0:T(8,128)S(1)} all-gather(f32[1,64,128]{2,1,0:T(8,128)S(1)} %dynamic-slice_subtract_fusion), channel_id=9, replica_groups=mesh['blk'=16,'grp'=2] {'blk'}, dimensions={1}, use_global_device_ids=true | all-gather | bytes 557056 | tf_op jit(solution)/shard_map/all_gather | solution.py:23
  773.3 0.5 fusion.36
  773.7 0.2 convolution_add_fusion
  774.0 1.1 maximum_add_fusion
  (25 shorter events, 0.2 us)
Async XLA Ops:
  7.2 191.0 %copy-start = (f32[8,64,1024]{2,1,0:T(8,128)S(1)}, f32[8,64,1024]{2,1,0:T(8,128)}, u32[]{:S(2)}) copy-start(f32[8,64,1024]{2,1,0:T(8,128)} %param.13) | copy-start | bytes 6291460
  7.2 151.6 %all-reduce.2.cloned.1.call-start = ((), (), s32[]{:S(2)}) async-start(), calls=%async_computation | async-start | bytes 524288 | tf_op jit(solution)/shard_map/psum | solution.py:61
  59.8 38.6 %copy-start.7 = (s32[2,24]{1,0:T(2,128)S(1)}, s32[2,24]{1,0:T(2,128)}, u32[]{:S(2)}) copy-start(s32[2,24]{1,0:T(2,128)} %param.10) | copy-start | bytes 580
  59.8 39.8 %copy-start.6 = (s32[8]{0:T(128)S(1)}, s32[8]{0:T(128)}, u32[]{:S(2)}) copy-start(s32[8]{0:T(128)} %param.11) | copy-start | bytes 100
  98.5 675.3 %copy-start.2 = (f32[2,1024,128]{2,1,0:T(8,128)}, f32[2,1024,128]{2,1,0:T(8,128)S(1)}, u32[]{:S(2)}) copy-start(f32[2,1024,128]{2,1,0:T(8,128)S(1)} %get-tuple-element.3) | copy-start | bytes 3145732
  198.2 44.7 %copy-start.5 = (f32[8,64,128]{2,1,0:T(8,128)S(1)}, f32[8,64,128]{2,1,0:T(8,128)}, u32[]{:S(2)}) copy-start(f32[8,64,128]{2,1,0:T(8,128)} %all-reduce.2.cloned.1.call-done) | copy-start | bytes 786436
  198.2 290.7 %copy-start.1 = (f32[8,8,64,1024]{3,2,1,0:T(8,128)S(1)}, f32[8,8,64,1024]{3,2,1,0:T(8,128)}, u32[]{:S(2)}) copy-start(f32[8,8,64,1024]{3,2,1,0:T(8,128)} %param.12) | copy-start | bytes 50331652
  733.2 40.8 %copy-start.3 = (f32[2,1024,128]{2,1,0:T(8,128)S(1)}, f32[2,1024,128]{2,1,0:T(8,128)}, u32[]{:S(2)}) copy-start(f32[2,1024,128]{2,1,0:T(8,128)} %param.9) | copy-start | bytes 3145732
  733.2 40.8 %copy-start.4 = (f32[2,1000,128]{2,1,0:T(8,128)S(1)}, f32[2,1000,128]{2,1,0:T(8,128)}, u32[]{:S(2)}) copy-start(f32[2,1000,128]{2,1,0:T(8,128)} %slice.42) | copy-start | bytes 3072004
Sparse Core Ops, SparseCore 0:
  99.8 18.6 all-reduce.1
